TPU v7x, 128 devices: a whole 4x4x4 slice. The times are simulated.
128 devices in a mesh: sample: 8 (over x, y_hi), gz: 16 (over z, y_lo, core).
Axes of the slice: x: 4, y: 4 (y_hi: 2, y_lo: 2; y = y_hi * 2 + y_lo), z: 4, core: 2. Of those that a mesh axis runs over, the one named last changes fastest.
Arguments:
- cubes: bfloat16 [16, 64, 32, 1024], P('sample', 'gz'), may hold values from -6 to 6
- weight_a: bfloat16 [27, 2048], replicated, may hold values from -0.21875 to 0.21875
- weight_b: bfloat16 [27, 8192], replicated, may hold values from -0.15625 to 0.15625
- cotangent: bfloat16 [16, 16, 8, 1024], P('sample', 'gz'), may hold values from -6 to 6
Outputs:
- input_grad: bfloat16 [16, 64, 32, 1024], P('sample', 'gz')
- weight_grad_a: float32 [27, 2048], replicated
- weight_grad_b: float32 [27, 8192], replicated
All inputs are finite; a program needn't handle non-finite values.
Results may differ from a plain program's by a relative error of at most 0.012.
Values may be sent and summed in bfloat16 or wider, within the bound.
A program may use at most 192 MiB of HBM per device.

v0:
```python
import functools

import jax
import jax.numpy as jnp
from jax import lax
from jax.experimental import pallas as pl
from jax.experimental.pallas import tpu as pltpu
from jax.sharding import PartitionSpec as P

C1, C2, C3 = 32, 64, 128
SIDE = 32
ZD = 4
CUBES = 2
BLOCKS = 9
F32, BF16 = jnp.float32, jnp.bfloat16
MESH = pl.DeviceIdType.MESH
ROWS_B = 1792
ROWS_A = 512


def iota(shape, dim):
    return lax.broadcasted_iota(jnp.int32, shape, dim)


def dot(a, b):
    return lax.dot_general(a, b, (((1,), (0,)), ((), ())), preferred_element_type=F32)


def dot_nt(a, b):
    return lax.dot_general(a, b, (((1,), (1,)), ((), ())), preferred_element_type=F32)


def rows_before(v):
    return jnp.where(iota(v.shape, 0) % 16 == 0, 0.0, pltpu.roll(v, 1, 0))


def rows_after(v):
    return jnp.where(iota(v.shape, 0) % 16 == 15, 0.0, pltpu.roll(v, v.shape[0] - 1, 0))


def lanes(start, size):
    return pl.ds(pl.multiple_of(start, 128), size)


def kernel(
    n_s, n_gz, x_ref, wa_ref, wb_ref, cot_ref, dx_ref, ga_ref, gb_ref,
    xa, ta, tb, tad, tbd, ds_a, pb, hb, ga, ht, gt, cs, da,
    xh, ph, hh, gh, sb, rb, eb, fb, sa, ra, ea, fa,
    halo_s, halo_r, rs_s, rs_r, ex_s, ex_r, ag_s, ag_r,
):
    me_s = lax.axis_index("sample")
    me_z = lax.axis_index("gz")
    low = lax.rem(me_z + n_gz - 1, n_gz)
    high = lax.rem(me_z + 1, n_gz)
    keep_low = (me_z > 0).astype(F32)
    keep_high = (me_z < n_gz - 1).astype(F32)

    barrier = pltpu.get_barrier_semaphore()

    @pl.loop(1, n_gz)
    def _(d):
        pl.semaphore_signal(barrier, inc=1, device_id=(me_s, lax.rem(me_z + d, n_gz)), device_id_type=MESH)

    @pl.loop(1, n_s)
    def _(d):
        pl.semaphore_signal(barrier, inc=1, device_id=(lax.rem(me_s + d, n_s), me_z), device_id_type=MESH)

    pl.semaphore_wait(barrier, n_gz + n_s - 2)

    def halo(stage, low_plane, high_plane, landing):
        pair = []
        for way, (src, peer) in enumerate(((high_plane, high), (low_plane, low))):
            copy = pltpu.make_async_remote_copy(
                src_ref=src, dst_ref=landing.at[way],
                send_sem=halo_s.at[stage, way], recv_sem=halo_r.at[stage, way],
                device_id=(me_s, peer), device_id_type=MESH,
            )
            copy.start()
            pair.append(copy)
        return pair

    halo_x = halo(0, x_ref.at[:, 0], x_ref.at[:, ZD - 1], xh)

    zero_a = jnp.zeros((C1, 128), BF16)
    zero_b = jnp.zeros((C2, 128), BF16)
    left = iota((C1, 128), 1) < C2

    def tap_a(zy, dx):
        if dx < -1 or dx > 1:
            return None
        return wa_ref[pl.ds(pl.multiple_of((zy * 3 + dx + 1) * C1, C1), C1), :]

    def tap_b(zy, dx):
        if dx < -1 or dx > 1:
            return zero_b
        return wb_ref[pl.ds(pl.multiple_of((zy * 3 + dx + 1) * C2, C2), C2), :]

    def two(zy, dx0, dx1):
        first, second = tap_a(zy, dx0), tap_a(zy, dx1)
        if first is None and second is None:
            return zero_a
        return jnp.where(left, zero_a if first is None else first, zero_a if second is None else second)

    @pl.loop(0, 9)
    def _(zy):
        base = zy * 256
        for p in range(8):
            for par in range(2):
                ta[pl.ds(pl.multiple_of(base + 32 * p, 32), 32), 128 * par:128 * par + 128] = two(zy, p - 2 - par, p - 4 - par)

    @pl.loop(0, 9)
    def _(zy):
        base = zy * 256
        for p in range(4):
            for q in range(2):
                tb[pl.ds(pl.multiple_of(base + 64 * p, 64), 64), 128 * q:128 * q + 128] = tap_b(zy, p - 1 - q)

    @pl.loop(0, 9)
    def _(s):
        for r in range(4):
            for p in range(6):
                tbd[64 * r:64 * r + 64, lanes(s * 768 + 128 * p, 128)] = tap_b(8 - s, r + 1 - p)

    @pl.loop(0, 9)
    def _(s):
        for r in range(8):
            for kk in range(3):
                for par in range(2):
                    dx = r + 2 - 4 * kk - par
                    tad[32 * r:32 * r + 32, lanes(s * 768 + 256 * kk + 128 * par, 128)] = two(8 - s, dx, dx - 2)

    spread_rows = (iota((64, SIDE), 1) == 2 * (iota((64, SIDE), 0) % 16) + iota((64, SIDE), 0) // 16 - 1).astype(BF16)
    spread_cot = (iota((16, 8), 0) // 2 == iota((16, 8), 1)).astype(BF16)
    natural = (iota((SIDE, SIDE), 1) == (iota((SIDE, SIDE), 0) % 2) * 16 + iota((SIDE, SIDE), 0) // 2).astype(BF16)
    edge = jnp.zeros((CUBES, ZD + 2, 64, 128), BF16)
    xa[:, :, :, 0:128] = edge
    xa[:, :, :, 1152:1280] = edge
    hb[:, :, :, :, 0:256] = jnp.zeros((CUBES, 4, 3, 16, 256), BF16)
    hb[:, :, :, :, 2304:2816] = jnp.zeros((CUBES, 4, 3, 16, 512), BF16)
    for b in range(CUBES):
        cs[b] = dot(spread_cot, cot_ref[b, 0]) * 0.125
        for z in range(ZD):
            xa[b, z + 1, :, 128:1152] = dot(spread_rows, x_ref[b, z]).astype(BF16)
    for copy in halo_x:
        copy.wait()
    for b in range(CUBES):
        xa[b, 0, :, 128:1152] = (dot(spread_rows, xh[0, b]) * keep_low).astype(BF16)
        xa[b, ZD + 1, :, 128:1152] = (dot(spread_rows, xh[1, b]) * keep_high).astype(BF16)

    @pl.loop(0, BLOCKS)
    def _(kk):
        window = [
            xa[:, dz:dz + ZD, 16 * dy:16 * dy + 32, lanes(128 * kk, 256)].reshape(256, 256)
            for dz in range(3) for dy in range(3)
        ]
        pre = dot(jnp.concatenate(window, axis=1), ta[...])
        place = 2 * kk - 1 + (iota((1, 128), 1) // C2)
        inside = ((place >= 0) & (place < SIDE // 2)).astype(F32) * 0.125
        s = 0.5 * jnp.tanh(0.5 * pre) + 0.5
        act = pre * s
        slope = s + act * (1.0 - s)
        ds_a[kk] = slope * jnp.concatenate([inside, inside], axis=1)
        act = (act[:, :128] + act[:, 128:]).reshape(CUBES, 2, 2, 2, 16, 128)
        pooled = (act[:, :, 0, 0] + act[:, :, 0, 1] + act[:, :, 1, 0] + act[:, :, 1, 1]).reshape(64, 128) * inside
        for dy, v in enumerate((rows_before(pooled), pooled, rows_after(pooled))):
            pb[:, 1:3, dy, :, lanes(128 * kk, 128)] = v.astype(BF16).reshape(CUBES, 2, 16, 128)

    halo_p = halo(1, pb.at[:, 1, 1], pb.at[:, 2, 1], ph)
    for copy in halo_p:
        copy.wait()
    for plane, way, keep in ((0, 0, keep_low), (3, 1, keep_high)):
        v = ph[way].astype(F32).reshape(32, 1152) * keep
        for dy, v in enumerate((rows_before(v), v, rows_after(v))):
            pb[:, plane, dy] = v.astype(BF16).reshape(CUBES, 16, 1152)

    @pl.loop(0, 2)
    def _(kc):
        stacks = []
        for i in range(4):
            stacks.append(jnp.concatenate([
                pb[:, dz:dz + 2, dy, :, lanes(512 * kc + 128 * i, 256)].reshape(64, 256)
                for dz in range(3) for dy in range(3)
            ], axis=1))
        pre = dot(jnp.concatenate(stacks, axis=0), tb[...])
        s = 0.5 * jnp.tanh(0.5 * pre) + 0.5
        slope = s + pre * s * (1.0 - s)
        grads = []
        for i in range(4):
            up = cs[:, :, lanes(512 * kc + 128 * i, 128)]
            up = jnp.concatenate([up, up], axis=2).reshape(CUBES, 1, 16, 256)
            h = (slope[64 * i:64 * i + 64].reshape(CUBES, 2, 16, 256) * up).reshape(64, 256)
            grads.append(h)
            for dy, v in enumerate((rows_before(h), h, rows_after(h))):
                hb[:, 1:3, dy, :, lanes(256 + 1024 * kc + 256 * i, 256)] = v.astype(BF16).reshape(CUBES, 2, 16, 256)
        ht[:, lanes(256 * kc, 256)] = jnp.concatenate(grads, axis=0).T.astype(BF16)

    halo_h = halo(2, hb.at[:, 1, 1, :, 256:2304], hb.at[:, 2, 1, :, 256:2304], hh)

    @pl.loop(0, 9)
    def _(zy):
        dz, dy = zy // 3, zy % 3
        window = jnp.concatenate([
            pb[:, pl.ds(dz, 2), dy, :, 128 * k:128 * k + 256].reshape(64, 256) for k in range(8)
        ], axis=0)
        full = dot(ht[...], window)
        diag = full[:128] + pltpu.roll(full[128:], 192, 1)
        sb[pl.ds(pl.multiple_of(zy * 192, 64), 192), :] = diag.T[:192].astype(BF16)

    sb[1728:ROWS_B, :] = jnp.zeros((ROWS_B - 1728, 128), BF16)

    def shard(ref, n, index):
        rows = ref.shape[0] // n
        return ref.at[pl.ds(pl.multiple_of(index * rows, 16), rows), :]

    def scatter_copy(which, send, land, d):
        peer = lax.rem(me_z + d, n_gz)
        return pltpu.make_async_remote_copy(
            src_ref=shard(send, n_gz, peer), dst_ref=land.at[me_z],
            send_sem=rs_s.at[which, d], recv_sem=rs_r.at[which, d],
            device_id=(me_s, peer), device_id_type=MESH,
        )

    def sample_copy(which, land, d):
        peer = lax.rem(me_s + d, n_s)
        return pltpu.make_async_remote_copy(
            src_ref=land.at[me_s], dst_ref=land.at[me_s],
            send_sem=ex_s.at[which, d], recv_sem=ex_r.at[which, d],
            device_id=(peer, me_z), device_id_type=MESH,
        )

    def gather_copy(which, full, d):
        peer = lax.rem(me_z + d, n_gz)
        return pltpu.make_async_remote_copy(
            src_ref=shard(full, n_gz, me_z), dst_ref=shard(full, n_gz, me_z),
            send_sem=ag_s.at[which, d], recv_sem=ag_r.at[which, d],
            device_id=(me_s, peer), device_id_type=MESH,
        )

    def start_all(make, n):
        @pl.loop(1, n)
        def _(d):
            make(d).start()

    def wait_all(make, n):
        @pl.loop(1, n)
        def _(d):
            make(d).wait()

    def scatter_start(which, send, land):
        start_all(functools.partial(scatter_copy, which, send, land), n_gz)

    def scatter_end(which, send, land, exchange):
        wait_all(functools.partial(scatter_copy, which, send, land), n_gz)
        rows = send.shape[0] // n_gz
        own = send[pl.ds(pl.multiple_of(me_z * rows, 16), rows), :]
        land[me_z] = own
        total = land[0].astype(F32)
        for t in range(1, n_gz):
            total = total + land[t].astype(F32)
        exchange[me_s] = total.astype(BF16)
        start_all(functools.partial(sample_copy, which, exchange), n_s)

    def exchange_end(which, exchange, full):
        wait_all(functools.partial(sample_copy, which, exchange), n_s)
        total = exchange[0].astype(F32)
        for t in range(1, n_s):
            total = total + exchange[t].astype(F32)
        rows = full.shape[0] // n_gz
        full[pl.ds(pl.multiple_of(me_z * rows, 16), rows), :] = (total * (1.0 / (CUBES * n_s))).astype(BF16)
        start_all(functools.partial(gather_copy, which, full), n_gz)

    scatter_start(0, sb, rb)

    for copy in halo_h:
        copy.wait()
    for plane, way, keep in ((0, 0, keep_low), (3, 1, keep_high)):
        v = hh[way].astype(F32).reshape(32, 2048) * keep
        for dy, v in enumerate((rows_before(v), v, rows_after(v))):
            hb[:, plane, dy, :, 256:2304] = v.astype(BF16).reshape(CUBES, 16, 2048)

    @pl.loop(0, 5)
    def _(j):
        gp = jnp.zeros((64, 256), F32)
        for sz in range(3):
            part = jnp.concatenate([
                hb[:, sz:sz + 2, sy, :, lanes(512 * j, 768)].reshape(64, 768) for sy in range(3)
            ], axis=1)
            gp = gp + dot_nt(part, tbd[:, 2304 * sz:2304 * sz + 2304])
        for half in range(2):
            @pl.when(2 * j + half < BLOCKS)
            def _():
                kk = 2 * j + half
                up = gp[:, 128 * half:128 * half + 128]
                up = jnp.concatenate([up, up], axis=1).reshape(CUBES, 2, 1, 1, 16, 256)
                g = ds_a[kk].reshape(CUBES, 2, 2, 2, 16, 256) * up
                gt[:, lanes(256 * kk, 256)] = g.reshape(256, 256).T.astype(BF16)
                g = g.reshape(CUBES, ZD, 2, 16, 256)
                even = g[:, :, 0].reshape(128, 256)
                odd = g[:, :, 1].reshape(128, 256)
                for group, v in enumerate((rows_before(odd), even, odd, rows_after(even))):
                    ga[:, 1:1 + ZD, 16 * group:16 * group + 16, lanes(256 * kk, 256)] = v.astype(BF16).reshape(CUBES, ZD, 16, 256)

    halo_g = halo(3, ga.at[:, 1, 16:48], ga.at[:, ZD, 16:48], gh)
    scatter_end(0, sb, rb, eb)

    @pl.loop(0, 9)
    def _(zy):
        dz, dy = zy // 3, zy % 3
        window = jnp.concatenate([
            xa[:, pl.ds(dz, ZD), pl.ds(pl.multiple_of(16 * dy, 16), 32), 128 * kk:128 * kk + 256].reshape(256, 256)
            for kk in range(BLOCKS)
        ], axis=0)
        full = dot(gt[...], window)
        total = jnp.zeros((64, 256), F32)
        for par in range(2):
            for pair in range(2):
                t = 2 * pair + par
                at = 128 * par + 64 * pair
                total = total + pltpu.roll(full[at:at + 64], 256 - 32 * (t + 1), 1)
        da[zy] = total[:, :128]

    da[9] = jnp.zeros((64, 128), F32)
    for i in range(5):
        both = jnp.concatenate([da[i], da[i + 5]], axis=0)
        sa[96 * i:96 * i + 96, :] = both.T[:96].astype(BF16)
    sa[480:ROWS_A, :] = jnp.zeros((ROWS_A - 480, 128), BF16)
    scatter_start(1, sa, ra)
    exchange_end(0, eb, fb)

    for copy in halo_g:
        copy.wait()
    for plane, way, keep in ((0, 0, keep_low), (ZD + 1, 1, keep_high)):
        even = gh[way, :, 0:16].astype(F32).reshape(32, 2304) * keep
        odd = gh[way, :, 16:32].astype(F32).reshape(32, 2304) * keep
        for group, v in enumerate((rows_before(odd), even, odd, rows_after(even))):
            ga[:, plane, 16 * group:16 * group + 16] = v.astype(BF16).reshape(CUBES, 16, 2304)

    def cubes_grad(j):
        total = jnp.zeros((256, 256), F32)
        for sz in range(3):
            part = jnp.concatenate([
                ga[:, sz:sz + ZD, 16 * sy:16 * sy + 32, lanes(512 * j, 768)].reshape(256, 768) for sy in range(3)
            ], axis=1)
            total = total + dot_nt(part, tad[:, 2304 * sz:2304 * sz + 2304])
        total = total.astype(BF16)
        for b in range(CUBES):
            for z in range(ZD):
                at = 32 * (ZD * b + z)
                dx_ref[b, z, :, lanes(256 * j, 256)] = dot(natural, total[at:at + 32]).astype(BF16)

    @pl.loop(0, 2)
    def _(j):
        cubes_grad(j)

    scatter_end(1, sa, ra, ea)

    @pl.loop(2, 4)
    def _(j):
        cubes_grad(j)

    exchange_end(1, ea, fa)
    wait_all(functools.partial(gather_copy, 0, fb), n_gz)
    gb_ref[...] = fb[0:1728].astype(F32)
    wait_all(functools.partial(gather_copy, 1, fa), n_gz)
    ga_ref[...] = fa[0:480].astype(F32)


def shards(n_s, n_gz, cubes, weight_a, weight_b, cotangent):
    wa = weight_a.reshape(27 * C1, C2)
    wa = jnp.concatenate([wa, wa], axis=1)
    wb = weight_b.reshape(27 * C2, C3)
    dma = pltpu.SemaphoreType.DMA
    vmem = pl.BlockSpec(memory_space=pltpu.VMEM)
    grad_x, grad_a, grad_b = pl.pallas_call(
        functools.partial(kernel, n_s, n_gz),
        out_shape=(
            jax.ShapeDtypeStruct((CUBES, ZD, SIDE, SIDE * C1), BF16),
            jax.ShapeDtypeStruct((480, 128), F32),
            jax.ShapeDtypeStruct((27 * C2, 128), F32),
        ),
        in_specs=[vmem] * 4,
        out_specs=(vmem,) * 3,
        scratch_shapes=[
            pltpu.VMEM((CUBES, ZD + 2, 64, 1280), BF16),
            pltpu.VMEM((2304, 256), BF16),
            pltpu.VMEM((2304, 256), BF16),
            pltpu.VMEM((256, 6912), BF16),
            pltpu.VMEM((256, 6912), BF16),
            pltpu.VMEM((BLOCKS, 256, 256), F32),
            pltpu.VMEM((CUBES, 4, 3, 16, 1152), BF16),
            pltpu.VMEM((CUBES, 4, 3, 16, 2816), BF16),
            pltpu.VMEM((CUBES, ZD + 2, 64, 2304), BF16),
            pltpu.VMEM((256, 512), BF16),
            pltpu.VMEM((256, 2304), BF16),
            pltpu.VMEM((CUBES, 16, 1024), F32),
            pltpu.VMEM((10, 64, 128), F32),
            pltpu.VMEM((2, CUBES, SIDE, 1024), BF16),
            pltpu.VMEM((2, CUBES, 16, 1152), BF16),
            pltpu.VMEM((2, CUBES, 16, 2048), BF16),
            pltpu.VMEM((2, CUBES, 32, 2304), BF16),
            pltpu.VMEM((ROWS_B, 128), BF16),
            pltpu.VMEM((n_gz, ROWS_B // n_gz, 128), BF16),
            pltpu.VMEM((n_s, ROWS_B // n_gz, 128), BF16),
            pltpu.VMEM((ROWS_B, 128), BF16),
            pltpu.VMEM((ROWS_A, 128), BF16),
            pltpu.VMEM((n_gz, ROWS_A // n_gz, 128), BF16),
            pltpu.VMEM((n_s, ROWS_A // n_gz, 128), BF16),
            pltpu.VMEM((ROWS_A, 128), BF16),
            dma((4, 2)), dma((4, 2)),
            dma((2, n_gz)), dma((2, n_gz)),
            dma((2, n_s)), dma((2, n_s)),
            dma((2, n_gz)), dma((2, n_gz)),
        ],
        compiler_params=pltpu.CompilerParams(
            collective_id=0, has_side_effects=True, vmem_limit_bytes=60 * 1024 * 1024
        ),
    )(cubes, wa, wb, cotangent)
    grad_a = jnp.concatenate([grad_a[:, :C2], grad_a[:384, C2:]], axis=0)
    return grad_x, grad_a.reshape(27, C1 * C2), grad_b.reshape(27, C2 * C3)


def solution(mesh):
    in_specs = (P("sample", "gz", None, None), P(), P(), P("sample", "gz", None, None))
    out_specs = (P("sample", "gz", None, None), P(), P())
    body = functools.partial(shards, mesh.shape["sample"], mesh.shape["gz"])
    return jax.shard_map(body, mesh=mesh, in_specs=in_specs, out_specs=out_specs, check_vma=False)
```

profile of v0, /device:TPU:1, one launch (start us, length us, event | category | flops | bytes accessed | tf_op | source)
XLA Modules:
  0.0 70.1 jit_solution(1206297392208731401)
XLA Ops:
  0.6 0.0 copy-start.3
  0.6 1.2 %reshape.18 = bf16[864,64]{1,0:T(8,128)(2,1)S(1)} reshape(bf16[27,2048]{1,0:T(8,128)(2,1)} %param.5) | data formatting | bytes 221184 | tf_op jit(solution)/shard_map/reshape | solution.py:369
  1.9 0.8 %pad_maximum_fusion.1.wa_ref = bf16[864,128]{1,0:T(8,128)(2,1)} fusion(bf16[864,64]{1,0:T(8,128)(2,1)S(1)} %reshape.18), kind=kLoop, calls=%fused_computation.1 | loop fusion | flops 442368 | bytes 331776 | tf_op jit(solution)/shard_map/concatenate | solution.py:370
  2.7 0.0 copy-done.3
  2.7 1.0 %reshape.19.wb_ref = bf16[1728,128]{1,0:T(8,128)(2,1)} reshape(bf16[27,8192]{1,0:T(8,128)(2,1)S(1)} %copy-done.3) | data formatting | bytes 884736 | tf_op jit(solution)/shard_map/reshape | solution.py:371
  3.7 62.1 %shard_map.67 = (bf16[2,4,32,1024]{3,2,1,0:T(8,128)(2,1)}, f32[480,128]{1,0:T(8,128)}, f32[1728,128]{1,0:T(8,128)}) custom-call(bf16[2,4,32,1024]{3,2,1,0:T(8,128)(2,1)} %x_ref.1, bf16[864,128]{1,0:T(8,128)(2,1)} %pad_maximum_fusion.1.wa_ref, bf16[1728,128]{1,0:T(8,128)(2,1)} %reshape.19.wb_ref, bf16[2,1,8,1024]{3,2,1,0:T(8,128)(2,1)} %cot_ref.1), custom_call_target="tpu_custom_call" | custom-call | tf_op jit(solution)/shard_map/pallas_call | solution.py:374
  65.8 0.0 copy-start.1
  65.8 1.1 %slice.7 = f32[384,64]{1,0:T(8,128)S(1)} slice(f32[480,128]{1,0:T(8,128)} %get-tuple-element.7), slice={[0:384], [64:128]} | slice | bytes 196608 | tf_op jit(solution)/shard_map/slice | solution.py:418
  66.9 0.0 copy-done.1
  66.9 0.0 copy-start
  67.0 0.9 %reshape.20 = f32[27,2048]{1,0:T(8,128)} reshape(f32[864,64]{1,0:T(8,128)S(1)} %pad_maximum_fusion) | data formatting | bytes 442368 | tf_op jit(solution)/shard_map/reshape | solution.py:419
  67.9 0.3 copy-done
  68.2 0.0 copy-start.2
  68.2 1.1 %reshape.21 = f32[27,8192]{1,0:T(8,128)} reshape(f32[1728,128]{1,0:T(8,128)S(1)} %copy-done) | data formatting | bytes 1769472 | tf_op jit(solution)/shard_map/reshape | solution.py:419
  69.3 0.0 copy-done.2
  69.3 0.8 %copy.8 = bf16[2,4,32,1024]{3,2,1,0:T(8,128)(2,1)} copy(bf16[2,4,32,1024]{3,2,1,0:T(8,128)(2,1)S(1)} %copy-done.2) | data formatting | bytes 1048576
  (1 shorter events, 0.0 us)
Async XLA Ops:
  0.6 2.0 %copy-start.3 = (bf16[27,8192]{1,0:T(8,128)(2,1)S(1)}, bf16[27,8192]{1,0:T(8,128)(2,1)}, u32[]{:S(2)}) copy-start(bf16[27,8192]{1,0:T(8,128)(2,1)} %param.6) | copy-start | bytes 1327108
  65.8 1.1 %copy-start.1 = (f32[480,128]{1,0:T(8,128)S(1)}, f32[480,128]{1,0:T(8,128)}, u32[]{:S(2)}) copy-start(f32[480,128]{1,0:T(8,128)} %get-tuple-element.7) | copy-start | bytes 737284
  66.9 1.2 %copy-start = (f32[1728,128]{1,0:T(8,128)S(1)}, f32[1728,128]{1,0:T(8,128)}, u32[]{:S(2)}) copy-start(f32[1728,128]{1,0:T(8,128)} %get-tuple-element.8) | copy-start | bytes 2654212
  68.2 1.1 %copy-start.2 = (bf16[2,4,32,1024]{3,2,1,0:T(8,128)(2,1)S(1)}, bf16[2,4,32,1024]{3,2,1,0:T(8,128)(2,1)}, u32[]{:S(2)}) copy-start(bf16[2,4,32,1024]{3,2,1,0:T(8,128)(2,1)} %get-tuple-element.12) | copy-start | bytes 1572868
where the time goes:
time: 70.3 us; the launch traced here: 70.1 us
  Pallas kernels  62.1 us (88%)
  local copies, waits for them, and re-layouts  6.45 us (9%)
  other arithmetic  0.85 us (1%)
    pallas_call x1, Pallas kernels, shards(): pl.pallas_call(functools.partial(kernel, n_s, n_gz), out_shape=(jax.Shape...  62.1 us
    reshape x2, local copies, waits for them, and re-layouts, shards(): return (grad_x, grad_a.reshape(27, C1 * C2), grad_b.reshape(27, C2 * C3))  1.99 us

commit v1 on v0

v1 whole, which is shorter than its diff:
```python
import functools

import jax
import jax.numpy as jnp
from jax import lax
from jax.experimental import pallas as pl
from jax.experimental.pallas import tpu as pltpu
from jax.sharding import PartitionSpec as P

C1, C2, C3 = 32, 64, 128
SIDE = 32
ZD = 4
CUBES = 2
BLOCKS = 9
F32, BF16 = jnp.float32, jnp.bfloat16
MESH = pl.DeviceIdType.MESH
ROWS_B = 1792
ROWS_A = 512


def iota(shape, dim):
    return lax.broadcasted_iota(jnp.int32, shape, dim)


def dot(a, b):
    return lax.dot_general(a, b, (((1,), (0,)), ((), ())), preferred_element_type=F32)


def dot_nt(a, b):
    return lax.dot_general(a, b, (((1,), (1,)), ((), ())), preferred_element_type=F32)


def rows_before(v):
    return jnp.where(iota(v.shape, 0) % 16 == 0, 0.0, pltpu.roll(v, 1, 0))


def rows_after(v):
    return jnp.where(iota(v.shape, 0) % 16 == 15, 0.0, pltpu.roll(v, v.shape[0] - 1, 0))


def lanes(start, size):
    return pl.ds(pl.multiple_of(start, 128), size)


def kernel(
    n_s, n_gz, x_hbm, wa_hbm, wb_hbm, cot_hbm, dx_hbm, ga_hbm, gb_hbm,
    x_ref, wa_ref, wb_ref, cot_ref, dx_ref, ga_ref, gb_ref,
    wa32, wb32, xa, ta, tb, tad, tbd, ds_a, pre_s, gp_s, pb, hb, ga, ht, gt, cs, da,
    xh, ph, hh, gh, sb, rb, eb, fb, sa, ra, ea, fa,
    load_s, store_s, halo_s, halo_r, rs_s, rs_r, ex_s, ex_r, ag_s, ag_r,
):
    me_s = lax.axis_index("sample")
    me_z = lax.axis_index("gz")
    low = lax.rem(me_z + n_gz - 1, n_gz)
    high = lax.rem(me_z + 1, n_gz)
    keep_low = (me_z > 0).astype(F32)
    keep_high = (me_z < n_gz - 1).astype(F32)

    barrier = pltpu.get_barrier_semaphore()

    @pl.loop(1, n_gz)
    def _(d):
        pl.semaphore_signal(barrier, inc=1, device_id=(me_s, lax.rem(me_z + d, n_gz)), device_id_type=MESH)

    @pl.loop(1, n_s)
    def _(d):
        pl.semaphore_signal(barrier, inc=1, device_id=(lax.rem(me_s + d, n_s), me_z), device_id_type=MESH)

    loads = [
        pltpu.make_async_copy(src, dst, load_s.at[i])
        for i, (src, dst) in enumerate(((wa_hbm, wa_ref), (wb_hbm, wb_ref), (x_hbm, x_ref), (cot_hbm, cot_ref)))
    ]
    for load in loads:
        load.start()

    def halo(stage, low_plane, high_plane, landing):
        pair = []
        for way, (src, peer) in enumerate(((high_plane, high), (low_plane, low))):
            copy = pltpu.make_async_remote_copy(
                src_ref=src, dst_ref=landing.at[way],
                send_sem=halo_s.at[stage, way], recv_sem=halo_r.at[stage, way],
                device_id=(me_s, peer), device_id_type=MESH,
            )
            copy.start()
            pair.append(copy)
        return pair

    half = iota((27, 128), 1) < C2
    loads[0].wait()

    @pl.loop(0, C1 // 2)
    def _(m):
        v = wa_ref[:, lanes(128 * m, 128)].astype(F32)
        w = pltpu.roll(v, C2, 1)
        wa32[pl.ds(2 * m, 27, stride=C1), :] = jnp.where(half, v, w)
        wa32[pl.ds(2 * m + 1, 27, stride=C1), :] = jnp.where(half, w, v)

    loads[1].wait()

    @pl.loop(0, C2)
    def _(i):
        wb32[pl.ds(i, 27, stride=C2), :] = wb_ref[:, lanes(128 * i, 128)].astype(F32)

    pl.semaphore_wait(barrier, n_gz + n_s - 2)
    halo_x = halo(0, x_hbm.at[:, 0], x_hbm.at[:, ZD - 1], xh)

    zero_a = jnp.zeros((C1, 128), BF16)
    zero_b = jnp.zeros((C2, 128), BF16)
    left = iota((C1, 128), 1) < C2

    def taps_a(zy):
        at = pl.multiple_of(zy * 3 * C1, C1)
        full = wa32[pl.ds(at, 3 * C1), :].astype(BF16)
        taps = [full[C1 * i:C1 * i + C1] for i in range(3)]

        def two(dx0, dx1):
            first = taps[dx0 + 1] if -1 <= dx0 <= 1 else zero_a
            second = taps[dx1 + 1] if -1 <= dx1 <= 1 else zero_a
            if first is second:
                return zero_a
            return jnp.where(left, first, second)

        return two

    def taps_b(zy):
        at = pl.multiple_of(zy * 3 * C2, C2)
        full = wb32[pl.ds(at, 3 * C2), :].astype(BF16)
        taps = [full[C2 * i:C2 * i + C2] for i in range(3)]
        return lambda dx: taps[dx + 1] if -1 <= dx <= 1 else zero_b

    @pl.loop(0, 9)
    def _(zy):
        dz = zy // 3
        base = (jnp.where(dz == 2, 2, 1 - dz) * 3 + zy % 3) * 256
        two = taps_a(zy)
        for p in range(8):
            for par in range(2):
                ta[pl.ds(pl.multiple_of(base + 32 * p, 32), 32), 128 * par:128 * par + 128] = two(p - 2 - par, p - 4 - par)

    spread_rows = (iota((64, SIDE), 1) == 2 * (iota((64, SIDE), 0) % 16) + iota((64, SIDE), 0) // 16 - 1).astype(BF16)
    spread_cot = (iota((16, 8), 0) // 2 == iota((16, 8), 1)).astype(BF16)
    natural = (iota((SIDE, SIDE), 1) == (iota((SIDE, SIDE), 0) % 2) * 16 + iota((SIDE, SIDE), 0) // 2).astype(BF16)
    edge = jnp.zeros((CUBES, ZD + 2, 64, 128), BF16)
    xa[:, :, :, 0:128] = edge
    xa[:, :, :, 1152:1280] = edge
    loads[2].wait()
    for b in range(CUBES):
        for z in range(ZD):
            xa[b, z + 1, :, 128:1152] = dot(spread_rows, x_ref[b, z]).astype(BF16)

    def x_windows(kt, planes):
        return jnp.concatenate([jnp.concatenate([
            xa[:, dz:dz + ZD, 16 * dy:16 * dy + 32, lanes(384 * kt + 128 * i, 256)].reshape(256, 256)
            for dz in planes for dy in range(3)
        ], axis=1) for i in range(3)], axis=0)

    @pl.loop(0, 3)
    def _(kt):
        part = dot(x_windows(kt, (1,)), ta[0:768])
        for i in range(3):
            ds_a[3 * kt + i] = part[256 * i:256 * i + 256]

    loads[3].wait()
    for b in range(CUBES):
        cs[b] = dot(spread_cot, cot_ref[b, 0]) * 0.125
    hb[:, :, :, :, 0:256] = jnp.zeros((CUBES, 4, 3, 16, 256), BF16)
    hb[:, :, :, :, 2304:2816] = jnp.zeros((CUBES, 4, 3, 16, 512), BF16)
    for copy in halo_x:
        copy.wait()
    for b in range(CUBES):
        xa[b, 0, :, 128:1152] = (dot(spread_rows, xh[0, b]) * keep_low).astype(BF16)
        xa[b, ZD + 1, :, 128:1152] = (dot(spread_rows, xh[1, b]) * keep_high).astype(BF16)

    @pl.loop(0, 3)
    def _(kt):
        part = dot(x_windows(kt, (0, 2)), ta[768:2304])
        for i in range(3):
            kk = 3 * kt + i
            pre = part[256 * i:256 * i + 256] + ds_a[kk]
            place = 2 * kk - 1 + (iota((1, 128), 1) // C2)
            inside = ((place >= 0) & (place < SIDE // 2)).astype(F32) * 0.125
            s = 0.5 * jnp.tanh(0.5 * pre) + 0.5
            act = pre * s
            slope = s + act * (1.0 - s)
            ds_a[kk] = slope * jnp.concatenate([inside, inside], axis=1)
            act = (act[:, :128] + act[:, 128:]).reshape(CUBES, 2, 2, 2, 16, 128)
            pooled = (act[:, :, 0, 0] + act[:, :, 0, 1] + act[:, :, 1, 0] + act[:, :, 1, 1]).reshape(64, 128) * inside
            for dy, v in enumerate((rows_before(pooled), pooled, rows_after(pooled))):
                pb[:, 1:3, dy, :, lanes(128 * kk, 128)] = v.astype(BF16).reshape(CUBES, 2, 16, 128)

    halo_p = halo(1, pb.at[:, 1, 1], pb.at[:, 2, 1], ph)

    @pl.loop(0, 9)
    def _(zy):
        base = zy * 256
        tap = taps_b(zy)
        for p in range(4):
            for q in range(2):
                tb[pl.ds(pl.multiple_of(base + 64 * p, 64), 64), 128 * q:128 * q + 128] = tap(p - 1 - q)

    def p_windows(planes):
        return jnp.concatenate([jnp.concatenate([
            pb[:, z, dy, :, 128 * k:128 * k + 256].reshape(32, 256) for z in planes for dy in range(3)
        ], axis=1) for k in range(8)], axis=0)

    window = p_windows((1, 2))
    pre_s[0] = dot(window, tb[768:2304])
    pre_s[1] = dot(window, tb[0:1536])

    @pl.loop(0, 9)
    def _(s):
        tap = taps_b(8 - s)
        for r in range(4):
            for p in range(6):
                tbd[64 * r:64 * r + 64, lanes(s * 768 + 128 * p, 128)] = tap(r + 1 - p)

    @pl.loop(0, 9)
    def _(s):
        two = taps_a(8 - s)
        for r in range(8):
            for kk in range(3):
                for par in range(2):
                    dx = r + 2 - 4 * kk - par
                    tad[32 * r:32 * r + 32, lanes(s * 768 + 256 * kk + 128 * par, 128)] = two(dx, dx - 2)

    for copy in halo_p:
        copy.wait()
    for plane, way, keep in ((0, 0, keep_low), (3, 1, keep_high)):
        v = ph[way].astype(F32).reshape(32, 1152) * keep
        for dy, v in enumerate((rows_before(v), v, rows_after(v))):
            pb[:, plane, dy] = v.astype(BF16).reshape(CUBES, 16, 1152)

    for zp in range(2):
        pre = pre_s[zp] + dot(p_windows((3 * zp,)), tb[1536 * zp:1536 * zp + 768])
        s = 0.5 * jnp.tanh(0.5 * pre) + 0.5
        slope = s + pre * s * (1.0 - s)
        grads = []
        for k in range(8):
            up = cs[:, :, 128 * k:128 * k + 128].reshape(32, 128)
            h = slope[32 * k:32 * k + 32] * jnp.concatenate([up, up], axis=1)
            grads.append(h)
            for dy, v in enumerate((rows_before(h), h, rows_after(h))):
                hb[:, 1 + zp, dy, :, 256 + 256 * k:512 + 256 * k] = v.astype(BF16).reshape(CUBES, 16, 256)
        ht[:, 256 * zp:256 * zp + 256] = jnp.concatenate(grads, axis=0).T.astype(BF16)

    halo_h = halo(2, hb.at[:, 1, 1, :, 256:2304], hb.at[:, 2, 1, :, 256:2304], hh)

    @pl.loop(0, 3)
    def _(dz):
        window = jnp.concatenate([jnp.concatenate([
            pb[:, dz + zp, dy, :, 128 * k:128 * k + 256].reshape(32, 256) for zp in range(2) for k in range(8)
        ], axis=0) for dy in range(3)], axis=1)
        all_dy = dot(ht[...], window)
        for dy in range(3):
            full = all_dy[:, 256 * dy:256 * dy + 256]
            diag = full[:128] + pltpu.roll(full[128:], 192, 1)
            sb[pl.ds(pl.multiple_of(dz * 576 + dy * 192, 64), 192), :] = diag.T[:192].astype(BF16)

    sb[1728:ROWS_B, :] = jnp.zeros((ROWS_B - 1728, 128), BF16)

    def shard(ref, n, index):
        rows = ref.shape[0] // n
        return ref.at[pl.ds(pl.multiple_of(index * rows, 16), rows), :]

    def scatter_copy(which, send, land, d):
        peer = lax.rem(me_z + d, n_gz)
        return pltpu.make_async_remote_copy(
            src_ref=shard(send, n_gz, peer), dst_ref=land.at[me_z],
            send_sem=rs_s.at[which, d], recv_sem=rs_r.at[which, d],
            device_id=(me_s, peer), device_id_type=MESH,
        )

    def sample_copy(which, land, d):
        peer = lax.rem(me_s + d, n_s)
        return pltpu.make_async_remote_copy(
            src_ref=land.at[me_s], dst_ref=land.at[me_s],
            send_sem=ex_s.at[which, d], recv_sem=ex_r.at[which, d],
            device_id=(peer, me_z), device_id_type=MESH,
        )

    def gather_copy(which, full, d):
        peer = lax.rem(me_z + d, n_gz)
        return pltpu.make_async_remote_copy(
            src_ref=shard(full, n_gz, me_z), dst_ref=shard(full, n_gz, me_z),
            send_sem=ag_s.at[which, d], recv_sem=ag_r.at[which, d],
            device_id=(me_s, peer), device_id_type=MESH,
        )

    def start_all(make, n):
        @pl.loop(1, n)
        def _(d):
            make(d).start()

    def wait_all(make, n):
        @pl.loop(1, n)
        def _(d):
            make(d).wait()

    def scatter_start(which, send, land):
        start_all(functools.partial(scatter_copy, which, send, land), n_gz)

    def scatter_end(which, send, land, exchange):
        wait_all(functools.partial(scatter_copy, which, send, land), n_gz)
        rows = send.shape[0] // n_gz
        own = send[pl.ds(pl.multiple_of(me_z * rows, 16), rows), :]
        land[me_z] = own
        total = land[0].astype(F32)
        for t in range(1, n_gz):
            total = total + land[t].astype(F32)
        exchange[me_s] = total.astype(BF16)
        start_all(functools.partial(sample_copy, which, exchange), n_s)

    def exchange_end(which, exchange, full):
        wait_all(functools.partial(sample_copy, which, exchange), n_s)
        total = exchange[0].astype(F32)
        for t in range(1, n_s):
            total = total + exchange[t].astype(F32)
        rows = full.shape[0] // n_gz
        full[pl.ds(pl.multiple_of(me_z * rows, 16), rows), :] = (total * (1.0 / (CUBES * n_s))).astype(BF16)
        start_all(functools.partial(gather_copy, which, full), n_gz)

    scatter_start(0, sb, rb)

    def h_windows(planes):
        return jnp.concatenate([jnp.concatenate([
            hb[:, z, sy, :, 512 * j:512 * j + 768].reshape(32, 768) for z in planes for sy in range(3)
        ], axis=1) for j in range(5)], axis=0)

    window = h_windows((1, 2))
    gp_s[0] = dot_nt(window, tbd[:, 2304:6912])
    gp_s[1] = dot_nt(window, tbd[:, 0:4608])

    for copy in halo_h:
        copy.wait()
    for plane, way, keep in ((0, 0, keep_low), (3, 1, keep_high)):
        v = hh[way].astype(F32).reshape(32, 2048) * keep
        for dy, v in enumerate((rows_before(v), v, rows_after(v))):
            hb[:, plane, dy, :, 256:2304] = v.astype(BF16).reshape(CUBES, 16, 2048)

    for zp in range(2):
        gp_s[zp] = gp_s[zp] + dot_nt(h_windows((3 * zp,)), tbd[:, 4608 * zp:4608 * zp + 2304])

    @pl.loop(0, BLOCKS)
    def _(kk):
        up = gp_s[:, pl.ds(pl.multiple_of((kk // 2) * 32, 32), 32), lanes(128 * (kk % 2), 128)]
        up = jnp.concatenate([up, up], axis=2).reshape(2, CUBES, 16, 256)
        g = []
        for b in range(CUBES):
            for zp in range(2):
                g.append((ds_a[kk, 128 * b + 64 * zp:128 * b + 64 * zp + 64].reshape(4, 16, 256) * up[zp, b][None]).reshape(64, 256))
        g = jnp.concatenate(g, axis=0)
        gt[:, lanes(256 * kk, 256)] = g.T.astype(BF16)
        g = g.reshape(CUBES, ZD, 2, 16, 256)
        even = g[:, :, 0].reshape(128, 256)
        odd = g[:, :, 1].reshape(128, 256)
        for group, v in enumerate((rows_before(odd), even, odd, rows_after(even))):
            ga[:, 1:1 + ZD, 16 * group:16 * group + 16, lanes(256 * kk, 256)] = v.astype(BF16).reshape(CUBES, ZD, 16, 256)

    halo_g = halo(3, ga.at[:, 1, 16:48], ga.at[:, ZD, 16:48], gh)

    def terms_a(dz):
        window = jnp.concatenate([jnp.concatenate([
            xa[:, pl.ds(dz, ZD), 16 * dy:16 * dy + 32, 128 * kk:128 * kk + 256].reshape(256, 256)
            for kk in range(BLOCKS)
        ], axis=0) for dy in range(3)], axis=1)
        all_dy = dot(gt[...], window)
        for dy in range(3):
            full = all_dy[:, 256 * dy:256 * dy + 256]
            total = jnp.zeros((64, 256), F32)
            for par in range(2):
                for pair in range(2):
                    t = 2 * pair + par
                    at = 128 * par + 64 * pair
                    total = total + pltpu.roll(full[at:at + 64], 256 - 32 * (t + 1), 1)
            total = total[:, :128]
            da[pl.ds(pl.multiple_of(dz * 288 + dy * 96, 32), 96), :] = jnp.concatenate([total, total], axis=0).T[:96]

    @pl.loop(0, 2)
    def _(dz):
        terms_a(dz)

    scatter_end(0, sb, rb, eb)
    terms_a(2)
    half = iota((ROWS_A, 128), 1) < C2
    da[864:1024, :] = jnp.zeros((160, 128), F32)
    sa[...] = jnp.where(half, da[0:512], da[512:1024]).astype(BF16)
    scatter_start(1, sa, ra)

    for copy in halo_g:
        copy.wait()
    for plane, way, keep in ((0, 0, keep_low), (ZD + 1, 1, keep_high)):
        even = gh[way, :, 0:16].astype(F32).reshape(32, 2304) * keep
        odd = gh[way, :, 16:32].astype(F32).reshape(32, 2304) * keep
        for group, v in enumerate((rows_before(odd), even, odd, rows_after(even))):
            ga[:, plane, 16 * group:16 * group + 16] = v.astype(BF16).reshape(CUBES, 16, 2304)

    exchange_end(0, eb, fb)

    stores = []

    def store(src, dst):
        copy = pltpu.make_async_copy(src, dst, store_s.at[len(stores)])
        copy.start()
        stores.append(copy)

    def cubes_grad(jj):
        part = jnp.concatenate([jnp.concatenate([
            ga[:, sz:sz + ZD, 16 * sy:16 * sy + 32, 1024 * jj + 512 * i:1024 * jj + 512 * i + 768].reshape(256, 768)
            for sz in range(3) for sy in range(3)
        ], axis=1) for i in range(2)], axis=0)
        total = dot_nt(part, tad[...]).astype(BF16)
        for i in range(2):
            for b in range(CUBES):
                for z in range(ZD):
                    at = 256 * i + 32 * (ZD * b + z)
                    dx_ref[b, z, :, 512 * jj + 256 * i:512 * jj + 256 * i + 256] = dot(natural, total[at:at + 32]).astype(BF16)

    cubes_grad(0)
    scatter_end(1, sa, ra, ea)
    cubes_grad(1)
    store(dx_ref, dx_hbm)
    exchange_end(1, ea, fa)

    wait_all(functools.partial(gather_copy, 0, fb), n_gz)
    wb32[...] = fb[0:1728].astype(F32)

    @pl.loop(0, C2)
    def _(i):
        gb_ref[:, lanes(128 * i, 128)] = wb32[pl.ds(i, 27, stride=C2), :]

    store(gb_ref, gb_hbm)
    wait_all(functools.partial(gather_copy, 1, fa), n_gz)
    wa32[0:ROWS_A] = fa[...].astype(F32)
    first = iota((16, 128), 1) < C2

    @pl.loop(0, C1 // 2)
    def _(m):
        v = wa32[pl.ds(2 * m, 16, stride=C1), :]
        w = wa32[pl.ds(2 * m + 1, 16, stride=C1), :]
        ga_ref[0:16, lanes(128 * m, 128)] = jnp.where(first, v, pltpu.roll(w, C2, 1))
        ga_ref[16:27, lanes(128 * m, 128)] = jnp.where(first, pltpu.roll(v, C2, 1), w)[:11]

    store(ga_ref, ga_hbm)
    for copy in stores:
        copy.wait()


def shards(n_s, n_gz, cubes, weight_a, weight_b, cotangent):
    dma = pltpu.SemaphoreType.DMA
    anywhere = pl.BlockSpec(memory_space=pl.ANY)
    ins = (cubes, weight_a, weight_b, cotangent)
    outs = (
        jax.ShapeDtypeStruct((CUBES, ZD, SIDE, SIDE * C1), BF16),
        jax.ShapeDtypeStruct((27, C1 * C2), F32),
        jax.ShapeDtypeStruct((27, C2 * C3), F32),
    )
    return pl.pallas_call(
        functools.partial(kernel, n_s, n_gz),
        out_shape=outs,
        in_specs=[anywhere] * 4,
        out_specs=(anywhere,) * 3,
        scratch_shapes=[pltpu.VMEM(v.shape, v.dtype) for v in ins + outs] + [
            pltpu.VMEM((27 * C1, 128), F32),
            pltpu.VMEM((27 * C2, 128), F32),
            pltpu.VMEM((CUBES, ZD + 2, 64, 1280), BF16),
            pltpu.VMEM((2304, 256), BF16),
            pltpu.VMEM((2304, 256), BF16),
            pltpu.VMEM((256, 6912), BF16),
            pltpu.VMEM((256, 6912), BF16),
            pltpu.VMEM((BLOCKS, 256, 256), F32),
            pltpu.VMEM((2, 256, 256), F32),
            pltpu.VMEM((2, 160, 256), F32),
            pltpu.VMEM((CUBES, 4, 3, 16, 1152), BF16),
            pltpu.VMEM((CUBES, 4, 3, 16, 2816), BF16),
            pltpu.VMEM((CUBES, ZD + 2, 64, 2304), BF16),
            pltpu.VMEM((256, 512), BF16),
            pltpu.VMEM((256, 2304), BF16),
            pltpu.VMEM((CUBES, 16, 1024), F32),
            pltpu.VMEM((1024, 128), F32),
            pltpu.VMEM((2, CUBES, SIDE, 1024), BF16),
            pltpu.VMEM((2, CUBES, 16, 1152), BF16),
            pltpu.VMEM((2, CUBES, 16, 2048), BF16),
            pltpu.VMEM((2, CUBES, 32, 2304), BF16),
            pltpu.VMEM((ROWS_B, 128), BF16),
            pltpu.VMEM((n_gz, ROWS_B // n_gz, 128), BF16),
            pltpu.VMEM((n_s, ROWS_B // n_gz, 128), BF16),
            pltpu.VMEM((ROWS_B, 128), BF16),
            pltpu.VMEM((ROWS_A, 128), BF16),
            pltpu.VMEM((n_gz, ROWS_A // n_gz, 128), BF16),
            pltpu.VMEM((n_s, ROWS_A // n_gz, 128), BF16),
            pltpu.VMEM((ROWS_A, 128), BF16),
            dma((4,)), dma((3,)),
            dma((4, 2)), dma((4, 2)),
            dma((2, n_gz)), dma((2, n_gz)),
            dma((2, n_s)), dma((2, n_s)),
            dma((2, n_gz)), dma((2, n_gz)),
        ],
        compiler_params=pltpu.CompilerParams(
            collective_id=0, has_side_effects=True, vmem_limit_bytes=60 * 1024 * 1024
        ),
    )(*ins)


def solution(mesh):
    in_specs = (P("sample", "gz", None, None), P(), P(), P("sample", "gz", None, None))
    out_specs = (P("sample", "gz", None, None), P(), P())
    body = functools.partial(shards, mesh.shape["sample"], mesh.shape["gz"])
    return jax.shard_map(body, mesh=mesh, in_specs=in_specs, out_specs=out_specs, check_vma=False)
```

time: 70.3 us -> 62.4 us (0.89)
  Pallas kernels: 62.1 us -> 57 us
  local copies, waits for them, and re-layouts: 6.45 us -> 4.6 us
  other arithmetic: 0.85 us -> 0 us
    pallas_call x1, Pallas kernels: 62.1 us -> 57 us  [shards(): pl.pallas_call(functools.partial(kernel, n_s, n_gz), out_shape=outs, in_s...]
    reshape x4 -> x0, local copies, waits for them, and re-layouts: 4.22 us -> none  [the longest x2 1.99 us: shards(): return (grad_x, grad_a.reshape(27, C1 * C2), grad_b.reshape(27, C2 * C3))]
    unnamed x9 -> x5, local copies, waits for them, and re-layouts: 1.13 us -> 4.6 us
    slice x1 -> x0, local copies, waits for them, and re-layouts: 1.1 us -> none  [shards(): grad_a = jnp.concatenate([grad_a[:, :C2], grad_a[:384, C2:]], axis=0)]
    concatenate x2 -> x0, other arithmetic: 0.85 us -> none  [the longest x1 0.82 us: shards(): wa = jnp.concatenate([wa, wa], axis=1)]
where the time goes in v1:
time: 62.4 us; the launch traced here: 62.2 us
  Pallas kernels  57 us (91%)
  local copies, waits for them, and re-layouts  4.6 us (7%)
  between operations  0.65 us (1%)
    pallas_call x1, Pallas kernels, shards(): pl.pallas_call(functools.partial(kernel, n_s, n_gz), out_shape=outs, in_s...  57 us
    unnamed x5, local copies, waits for them, and re-layouts  4.6 us

profile of v1, /device:TPU:1, one launch (start us, length us, event | category | flops | bytes accessed | tf_op | source)
XLA Modules:
  0.0 62.2 jit_solution(16731469034628749084)
XLA Ops:
  0.6 57.0 %shard_map.67 = (bf16[2,4,32,1024]{3,2,1,0:T(8,128)(2,1)}, f32[27,2048]{1,0:T(8,128)}, f32[27,8192]{1,0:T(8,128)}) custom-call(bf16[2,4,32,1024]{3,2,1,0:T(8,128)(2,1)} %x_hbm.1, bf16[27,2048]{1,0:T(8,128)(2,1)} %wa_hbm.1, bf16[27,8192]{1,0:T(8,128)(2,1)} %wb_hbm.1, bf16[2,1,8,1024]{3,2,1,0:T(8,128)(2,1)} %cot_hbm.1), custom_call_target="tpu_custom_call" | custom-call | tf_op jit(solution)/shard_map/pallas_call | solution.py:457
  57.6 0.0 copy-start
  57.6 2.0 %copy.10 = bf16[2,4,32,1024]{3,2,1,0:T(8,128)(2,1)} copy(bf16[2,4,32,1024]{3,2,1,0:T(8,128)(2,1)} %get-tuple-element.6) | data formatting | bytes 1048576
  59.6 1.7 %copy.11 = f32[27,2048]{1,0:T(8,128)} copy(f32[27,2048]{1,0:T(8,128)} %get-tuple-element.7) | data formatting | bytes 442368
  61.3 0.0 copy-done
  61.3 1.0 %copy.12 = f32[27,8192]{1,0:T(8,128)} copy(f32[27,8192]{1,0:T(8,128)S(1)} %copy-done) | data formatting | bytes 1769472
Async XLA Ops:
  57.6 3.6 %copy-start = (f32[27,8192]{1,0:T(8,128)S(1)}, f32[27,8192]{1,0:T(8,128)}, u32[]{:S(2)}) copy-start(f32[27,8192]{1,0:T(8,128)} %get-tuple-element.8) | copy-start | bytes 2654212

commit v2 on v1

--- a/solution.py
+++ b/solution.py
@@ -15,6 +15,8 @@
 F32, BF16 = jnp.float32, jnp.bfloat16
 MESH = pl.DeviceIdType.MESH
 ROWS_B = 1792
+HALF_B = 896
+WIDE_B = 1024
 ROWS_A = 512
 
 
@@ -46,8 +48,8 @@
     n_s, n_gz, x_hbm, wa_hbm, wb_hbm, cot_hbm, dx_hbm, ga_hbm, gb_hbm,
     x_ref, wa_ref, wb_ref, cot_ref, dx_ref, ga_ref, gb_ref,
     wa32, wb32, xa, ta, tb, tad, tbd, ds_a, pre_s, gp_s, pb, hb, ga, ht, gt, cs, da,
-    xh, ph, hh, gh, sb, rb, eb, fb, sa, ra, ea, fa,
-    load_s, store_s, halo_s, halo_r, rs_s, rs_r, ex_s, ex_r, ag_s, ag_r,
+    xh, ph, hh, gh, sb, cb, hs, rb, eb, fh, fo, sa, ra, ea, fa,
+    load_s, store_s, halo_s, halo_r, core_s, core_r, rs_s, rs_r, ex_s, ex_r, ag_s, ag_r,
 ):
     me_s = lax.axis_index("sample")
     me_z = lax.axis_index("gz")
@@ -56,7 +58,28 @@
     keep_low = (me_z > 0).astype(F32)
     keep_high = (me_z < n_gz - 1).astype(F32)
 
+    core, y_lo, at_z = me_z % 2, (me_z // 2) % 2, me_z // 4
+    at_x, y_hi = me_s // 2, me_s % 2
+    n_e = n_s // 2
+    mine = (core * at_x + (1 - core) * at_z) * 4 + y_hi * 2 + y_lo
+    last = core * at_z + (1 - core) * at_x
+
+    def in_group(t):
+        a, y = t // 4, t % 4
+        to_x = core * a + (1 - core) * at_x
+        to_z = (1 - core) * a + core * at_z
+        return (to_x * 2 + y // 2, to_z * 4 + (y % 2) * 2 + core)
+
+    def in_line(e):
+        to_x = core * at_x + (1 - core) * e
+        to_z = (1 - core) * at_z + core * e
+        return (to_x * 2 + y_hi, to_z * 4 + y_lo * 2 + core)
+
     barrier = pltpu.get_barrier_semaphore()
+
+    @pl.loop(1, n_gz)
+    def _(d):
+        pl.semaphore_signal(barrier, inc=1, device_id=in_group(lax.rem(mine + d, n_gz)), device_id_type=MESH)
 
     @pl.loop(1, n_gz)
     def _(d):
@@ -101,7 +124,7 @@
     def _(i):
         wb32[pl.ds(i, 27, stride=C2), :] = wb_ref[:, lanes(128 * i, 128)].astype(F32)
 
-    pl.semaphore_wait(barrier, n_gz + n_s - 2)
+    pl.semaphore_wait(barrier, 2 * n_gz + n_s - 3)
     halo_x = halo(0, x_hbm.at[:, 0], x_hbm.at[:, ZD - 1], xh)
 
     zero_a = jnp.zeros((C1, 128), BF16)
@@ -257,6 +280,7 @@
             sb[pl.ds(pl.multiple_of(dz * 576 + dy * 192, 64), 192), :] = diag.T[:192].astype(BF16)
 
     sb[1728:ROWS_B, :] = jnp.zeros((ROWS_B - 1728, 128), BF16)
+    hs[HALF_B:, :] = jnp.zeros((WIDE_B - HALF_B, 128), BF16)
 
     def shard(ref, n, index):
         rows = ref.shape[0] // n
@@ -319,7 +343,79 @@
         full[pl.ds(pl.multiple_of(me_z * rows, 16), rows), :] = (total * (1.0 / (CUBES * n_s))).astype(BF16)
         start_all(functools.partial(gather_copy, which, full), n_gz)
 
-    scatter_start(0, sb, rb)
+    def half_of(ref, which):
+        return ref.at[pl.ds(pl.multiple_of(which * HALF_B, 128), HALF_B), :]
+
+    part = WIDE_B // n_gz
+
+    def part_of(ref, t):
+        return ref.at[pl.ds(pl.multiple_of(t * part, 64), part), :]
+
+    def core_copy(stage, src, dst):
+        return pltpu.make_async_remote_copy(
+            src_ref=src, dst_ref=dst, send_sem=core_s.at[stage], recv_sem=core_r.at[stage],
+            device_id=(me_s, me_z + 1 - 2 * core), device_id_type=MESH,
+        )
+
+    def group_copy(d):
+        peer = lax.rem(mine + d, n_gz)
+        return pltpu.make_async_remote_copy(
+            src_ref=part_of(hs, peer), dst_ref=rb.at[mine], send_sem=rs_s.at[0, d], recv_sem=rs_r.at[0, d],
+            device_id=in_group(peer), device_id_type=MESH,
+        )
+
+    def line_copy(d):
+        return pltpu.make_async_remote_copy(
+            src_ref=eb.at[last], dst_ref=eb.at[last], send_sem=ex_s.at[0, d], recv_sem=ex_r.at[0, d],
+            device_id=in_line(lax.rem(last + d, n_e)), device_id_type=MESH,
+        )
+
+    def back_copy(d):
+        return pltpu.make_async_remote_copy(
+            src_ref=part_of(fh, mine), dst_ref=part_of(fh, mine), send_sem=ag_s.at[0, d], recv_sem=ag_r.at[0, d],
+            device_id=in_group(lax.rem(mine + d, n_gz)), device_id_type=MESH,
+        )
+
+    def reduce_b0():
+        swap = core_copy(0, half_of(sb, 1 - core), cb)
+        swap.start()
+        return swap
+
+    def reduce_b1(swap):
+        swap.wait()
+        own = sb[pl.ds(pl.multiple_of(core * HALF_B, 128), HALF_B), :]
+        hs[0:HALF_B] = (own.astype(F32) + cb[...].astype(F32)).astype(BF16)
+        start_all(group_copy, n_gz)
+
+    def reduce_b2():
+        wait_all(group_copy, n_gz)
+        rb[mine] = hs[pl.ds(pl.multiple_of(mine * part, 64), part), :]
+        total = rb[0].astype(F32)
+        for t in range(1, n_gz):
+            total = total + rb[t].astype(F32)
+        eb[last] = total.astype(BF16)
+        start_all(line_copy, n_e)
+
+    def reduce_b3():
+        wait_all(line_copy, n_e)
+        total = eb[0].astype(F32)
+        for t in range(1, n_e):
+            total = total + eb[t].astype(F32)
+        fh[pl.ds(pl.multiple_of(mine * part, 64), part), :] = (total * (1.0 / (CUBES * n_s))).astype(BF16)
+        start_all(back_copy, n_gz)
+
+    def reduce_b4():
+        wait_all(back_copy, n_gz)
+        swap = core_copy(1, fh.at[0:HALF_B], fo)
+        swap.start()
+        wb32[pl.ds(pl.multiple_of(core * HALF_B, 128), HALF_B), :] = fh[0:HALF_B].astype(F32)
+        return swap
+
+    def reduce_b5(swap):
+        swap.wait()
+        wb32[pl.ds(pl.multiple_of((1 - core) * HALF_B, 128), HALF_B), :] = fo[...].astype(F32)
+
+    swap = reduce_b0()
 
     def h_windows(planes):
         return jnp.concatenate([jnp.concatenate([
@@ -330,6 +426,7 @@
     gp_s[0] = dot_nt(window, tbd[:, 2304:6912])
     gp_s[1] = dot_nt(window, tbd[:, 0:4608])
 
+    reduce_b1(swap)
     for copy in halo_h:
         copy.wait()
     for plane, way, keep in ((0, 0, keep_low), (3, 1, keep_high)):
@@ -375,16 +472,15 @@
             total = total[:, :128]
             da[pl.ds(pl.multiple_of(dz * 288 + dy * 96, 32), 96), :] = jnp.concatenate([total, total], axis=0).T[:96]
 
-    @pl.loop(0, 2)
+    @pl.loop(0, 3)
     def _(dz):
         terms_a(dz)
 
-    scatter_end(0, sb, rb, eb)
-    terms_a(2)
     half = iota((ROWS_A, 128), 1) < C2
     da[864:1024, :] = jnp.zeros((160, 128), F32)
     sa[...] = jnp.where(half, da[0:512], da[512:1024]).astype(BF16)
     scatter_start(1, sa, ra)
+    reduce_b2()
 
     for copy in halo_g:
         copy.wait()
@@ -394,7 +490,6 @@
         for group, v in enumerate((rows_before(odd), even, odd, rows_after(even))):
             ga[:, plane, 16 * group:16 * group + 16] = v.astype(BF16).reshape(CUBES, 16, 2304)
 
-    exchange_end(0, eb, fb)
 
     stores = []
 
@@ -416,13 +511,13 @@
                     dx_ref[b, z, :, 512 * jj + 256 * i:512 * jj + 256 * i + 256] = dot(natural, total[at:at + 32]).astype(BF16)
 
     cubes_grad(0)
+    reduce_b3()
     scatter_end(1, sa, ra, ea)
     cubes_grad(1)
     store(dx_ref, dx_hbm)
     exchange_end(1, ea, fa)
 
-    wait_all(functools.partial(gather_copy, 0, fb), n_gz)
-    wb32[...] = fb[0:1728].astype(F32)
+    reduce_b5(reduce_b4())
 
     @pl.loop(0, C2)
     def _(i):
@@ -442,6 +537,22 @@
 
     store(ga_ref, ga_hbm)
     for copy in stores:
+        copy.wait()
+
+
+def pass_on(dx_in, ga_in, gb_in, dx_out, ga_out, gb_out, dx_ref, ga_ref, gb_ref, in_s, out_s):
+    near, far = pl.ds(0, 4096), pl.ds(4096, 4096)
+    pieces = [(dx_in.at[b], dx_ref.at[b], dx_out.at[b]) for b in range(CUBES)]
+    pieces += [(gb_in.at[:, w], gb_ref.at[:, w], gb_out.at[:, w]) for w in (near, far)]
+    pieces.append((ga_in, ga_ref, ga_out))
+    taken = [pltpu.make_async_copy(src, via, in_s.at[i]) for i, (src, via, _) in enumerate(pieces)]
+    given = [pltpu.make_async_copy(via, dst, out_s.at[i]) for i, (_, via, dst) in enumerate(pieces)]
+    for copy in taken:
+        copy.start()
+    for arrive, leave in zip(taken, given):
+        arrive.wait()
+        leave.start()
+    for copy in given:
         copy.wait()
 
 
@@ -454,14 +565,14 @@
         jax.ShapeDtypeStruct((27, C1 * C2), F32),
         jax.ShapeDtypeStruct((27, C2 * C3), F32),
     )
-    return pl.pallas_call(
+    results = pl.pallas_call(
         functools.partial(kernel, n_s, n_gz),
         out_shape=outs,
         in_specs=[anywhere] * 4,
         out_specs=(anywhere,) * 3,
         scratch_shapes=[pltpu.VMEM(v.shape, v.dtype) for v in ins + outs] + [
             pltpu.VMEM((27 * C1, 128), F32),
-            pltpu.VMEM((27 * C2, 128), F32),
+            pltpu.VMEM((ROWS_B, 128), F32),
             pltpu.VMEM((CUBES, ZD + 2, 64, 1280), BF16),
             pltpu.VMEM((2304, 256), BF16),
             pltpu.VMEM((2304, 256), BF16),
@@ -482,15 +593,18 @@
             pltpu.VMEM((2, CUBES, 16, 2048), BF16),
             pltpu.VMEM((2, CUBES, 32, 2304), BF16),
             pltpu.VMEM((ROWS_B, 128), BF16),
-            pltpu.VMEM((n_gz, ROWS_B // n_gz, 128), BF16),
-            pltpu.VMEM((n_s, ROWS_B // n_gz, 128), BF16),
-            pltpu.VMEM((ROWS_B, 128), BF16),
+            pltpu.VMEM((HALF_B, 128), BF16),
+            pltpu.VMEM((WIDE_B, 128), BF16),
+            pltpu.VMEM((n_gz, WIDE_B // n_gz, 128), BF16),
+            pltpu.VMEM((n_s // 2, WIDE_B // n_gz, 128), BF16),
+            pltpu.VMEM((WIDE_B, 128), BF16),
+            pltpu.VMEM((HALF_B, 128), BF16),
             pltpu.VMEM((ROWS_A, 128), BF16),
             pltpu.VMEM((n_gz, ROWS_A // n_gz, 128), BF16),
             pltpu.VMEM((n_s, ROWS_A // n_gz, 128), BF16),
             pltpu.VMEM((ROWS_A, 128), BF16),
             dma((4,)), dma((3,)),
-            dma((4, 2)), dma((4, 2)),
+            dma((4, 2)), dma((4, 2)), dma((2,)), dma((2,)),
             dma((2, n_gz)), dma((2, n_gz)),
             dma((2, n_s)), dma((2, n_s)),
             dma((2, n_gz)), dma((2, n_gz)),
@@ -499,6 +613,13 @@
             collective_id=0, has_side_effects=True, vmem_limit_bytes=60 * 1024 * 1024
         ),
     )(*ins)
+    return pl.pallas_call(
+        pass_on,
+        out_shape=outs,
+        in_specs=[anywhere] * 3,
+        out_specs=(anywhere,) * 3,
+        scratch_shapes=[pltpu.VMEM(v.shape, v.dtype) for v in outs] + [dma((5,)), dma((5,))],
+    )(*results)
 
 
 def solution(mesh):

time: 62.4 us -> 59.1 us (0.947)
  local copies, waits for them, and re-layouts: 4.6 us -> 0 us
  Pallas kernels: 57 us -> 58.3 us
    unnamed x5 -> x0, local copies, waits for them, and re-layouts: 4.6 us -> none
    pallas_call x0 -> x1, Pallas kernels: none -> 2.34 us  [shards(): pl.pallas_call(pass_on, out_shape=outs, in_specs=[anywhere] * 3, out_spec...]
    pallas_call x1, Pallas kernels: 57 us -> 55.9 us  [shards(): pl.pallas_call(functools.partial(kernel, n_s, n_gz), out_shape=outs, in_s...]
where the time goes in v2:
time: 59.1 us; the launch traced here: 58.9 us
  Pallas kernels  58.3 us (99%)
  between operations  0.64 us (1%)
    pallas_call x1, Pallas kernels, shards(): pl.pallas_call(functools.partial(kernel, n_s, n_gz), out_shape=outs, in_s...  55.9 us
    pallas_call x1, Pallas kernels, shards(): pl.pallas_call(pass_on, out_shape=outs, in_specs=[anywhere] * 3, out_spec...  2.34 us

profile of v2, /device:TPU:1, one launch (start us, length us, event | category | flops | bytes accessed | tf_op | source)
XLA Modules:
  0.0 58.9 jit_solution(16281701231474388838)
XLA Ops:
  0.6 55.9 %shard_map.67 = (bf16[2,4,32,1024]{3,2,1,0:T(8,128)(2,1)}, f32[27,2048]{1,0:T(8,128)}, f32[27,8192]{1,0:T(8,128)}) custom-call(bf16[2,4,32,1024]{3,2,1,0:T(8,128)(2,1)} %x_hbm.1, bf16[27,2048]{1,0:T(8,128)(2,1)} %wa_hbm.1, bf16[27,8192]{1,0:T(8,128)(2,1)} %wb_hbm.1, bf16[2,1,8,1024]{3,2,1,0:T(8,128)(2,1)} %cot_hbm.1), custom_call_target="tpu_custom_call" | custom-call | tf_op jit(solution)/shard_map/pallas_call | solution.py:568
  56.6 2.3 %shard_map.68 = (bf16[2,4,32,1024]{3,2,1,0:T(8,128)(2,1)}, f32[27,2048]{1,0:T(8,128)}, f32[27,8192]{1,0:T(8,128)}) custom-call(bf16[2,4,32,1024]{3,2,1,0:T(8,128)(2,1)} %get-tuple-element.6.dx_in, f32[27,2048]{1,0:T(8,128)} %get-tuple-element.7.ga_in, f32[27,8192]{1,0:T(8,128)} %get-tuple-element.8.gb_in), custom_call_target="tpu_custom_call" | custom-call | tf_op jit(solution)/shard_map/pallas_call | solution.py:616

commit v3 on v2

--- a/solution.py
+++ b/solution.py
@@ -240,11 +240,13 @@
     @pl.loop(0, 9)
     def _(s):
         two = taps_a(8 - s)
+        sz = s // 3
+        base = (jnp.where(sz == 2, 2, 1 - sz) * 3 + s % 3) * 768
         for r in range(8):
             for kk in range(3):
                 for par in range(2):
                     dx = r + 2 - 4 * kk - par
-                    tad[32 * r:32 * r + 32, lanes(s * 768 + 256 * kk + 128 * par, 128)] = two(dx, dx - 2)
+                    tad[32 * r:32 * r + 32, lanes(base + 256 * kk + 128 * par, 128)] = two(dx, dx - 2)
 
     for copy in halo_p:
         copy.wait()
@@ -264,7 +266,7 @@
             grads.append(h)
             for dy, v in enumerate((rows_before(h), h, rows_after(h))):
                 hb[:, 1 + zp, dy, :, 256 + 256 * k:512 + 256 * k] = v.astype(BF16).reshape(CUBES, 16, 256)
-        ht[:, 256 * zp:256 * zp + 256] = jnp.concatenate(grads, axis=0).T.astype(BF16)
+        ht[:, 256 * zp:256 * zp + 256] = jnp.concatenate(grads, axis=0).astype(BF16).T
 
     halo_h = halo(2, hb.at[:, 1, 1, :, 256:2304], hb.at[:, 2, 1, :, 256:2304], hh)
 
@@ -277,7 +279,7 @@
         for dy in range(3):
             full = all_dy[:, 256 * dy:256 * dy + 256]
             diag = full[:128] + pltpu.roll(full[128:], 192, 1)
-            sb[pl.ds(pl.multiple_of(dz * 576 + dy * 192, 64), 192), :] = diag.T[:192].astype(BF16)
+            sb[pl.ds(pl.multiple_of(dz * 576 + dy * 192, 64), 192), :] = diag.astype(BF16).T[:192]
 
     sb[1728:ROWS_B, :] = jnp.zeros((ROWS_B - 1728, 128), BF16)
     hs[HALF_B:, :] = jnp.zeros((WIDE_B - HALF_B, 128), BF16)
@@ -446,7 +448,7 @@
             for zp in range(2):
                 g.append((ds_a[kk, 128 * b + 64 * zp:128 * b + 64 * zp + 64].reshape(4, 16, 256) * up[zp, b][None]).reshape(64, 256))
         g = jnp.concatenate(g, axis=0)
-        gt[:, lanes(256 * kk, 256)] = g.T.astype(BF16)
+        gt[:, lanes(256 * kk, 256)] = g.astype(BF16).T
         g = g.reshape(CUBES, ZD, 2, 16, 256)
         even = g[:, :, 0].reshape(128, 256)
         odd = g[:, :, 1].reshape(128, 256)
@@ -480,8 +482,36 @@
     da[864:1024, :] = jnp.zeros((160, 128), F32)
     sa[...] = jnp.where(half, da[0:512], da[512:1024]).astype(BF16)
     scatter_start(1, sa, ra)
+    stores = []
+
+    def store(src, dst):
+        copy = pltpu.make_async_copy(src, dst, store_s.at[len(stores)])
+        copy.start()
+        stores.append(copy)
+
+    def g_windows(jj, planes):
+        return jnp.concatenate([jnp.concatenate([
+            ga[:, sz:sz + ZD, 16 * sy:16 * sy + 32, 1024 * jj + 512 * i:1024 * jj + 512 * i + 768].reshape(256, 768)
+            for sz in planes for sy in range(3)
+        ], axis=1) for i in range(2)], axis=0)
+
+    def middle(jj):
+        part = dot_nt(g_windows(jj, (1,)), tad[:, 0:2304])
+        for i in range(2):
+            ds_a[2 * jj + i] = part[256 * i:256 * i + 256]
+
+    def cubes_grad(jj):
+        part = dot_nt(g_windows(jj, (0, 2)), tad[:, 2304:6912])
+        for i in range(2):
+            total = (part[256 * i:256 * i + 256] + ds_a[2 * jj + i]).astype(BF16)
+            for b in range(CUBES):
+                for z in range(ZD):
+                    at = 32 * (ZD * b + z)
+                    dx_ref[b, z, :, 512 * jj + 256 * i:512 * jj + 256 * i + 256] = dot(natural, total[at:at + 32]).astype(BF16)
+
+    middle(0)
     reduce_b2()
-
+    middle(1)
     for copy in halo_g:
         copy.wait()
     for plane, way, keep in ((0, 0, keep_low), (ZD + 1, 1, keep_high)):
@@ -491,32 +521,12 @@
             ga[:, plane, 16 * group:16 * group + 16] = v.astype(BF16).reshape(CUBES, 16, 2304)
 
 
-    stores = []
-
-    def store(src, dst):
-        copy = pltpu.make_async_copy(src, dst, store_s.at[len(stores)])
-        copy.start()
-        stores.append(copy)
-
-    def cubes_grad(jj):
-        part = jnp.concatenate([jnp.concatenate([
-            ga[:, sz:sz + ZD, 16 * sy:16 * sy + 32, 1024 * jj + 512 * i:1024 * jj + 512 * i + 768].reshape(256, 768)
-            for sz in range(3) for sy in range(3)
-        ], axis=1) for i in range(2)], axis=0)
-        total = dot_nt(part, tad[...]).astype(BF16)
-        for i in range(2):
-            for b in range(CUBES):
-                for z in range(ZD):
-                    at = 256 * i + 32 * (ZD * b + z)
-                    dx_ref[b, z, :, 512 * jj + 256 * i:512 * jj + 256 * i + 256] = dot(natural, total[at:at + 32]).astype(BF16)
-
     cubes_grad(0)
+    scatter_end(1, sa, ra, ea)
     reduce_b3()
-    scatter_end(1, sa, ra, ea)
     cubes_grad(1)
     store(dx_ref, dx_hbm)
     exchange_end(1, ea, fa)
-
     reduce_b5(reduce_b4())
 
     @pl.loop(0, C2)

time: 59.1 us -> 57.3 us (0.970)
  Pallas kernels: 58.3 us -> 56.5 us
    pallas_call x1, Pallas kernels: 55.9 us -> 54.2 us  [shards(): pl.pallas_call(functools.partial(kernel, n_s, n_gz), out_shape=outs, in_s...]
where the time goes in v3:
time: 57.3 us; the launch traced here: 57.1 us
  Pallas kernels  56.5 us (99%)
  between operations  0.64 us (1%)
    pallas_call x1, Pallas kernels, shards(): pl.pallas_call(functools.partial(kernel, n_s, n_gz), out_shape=outs, in_s...  54.2 us
    pallas_call x1, Pallas kernels, shards(): pl.pallas_call(pass_on, out_shape=outs, in_specs=[anywhere] * 3, out_spec...  2.34 us

profile of v3, /device:TPU:1, one launch (start us, length us, event | category | flops | bytes accessed | tf_op | source)
XLA Modules:
  0.0 57.1 jit_solution(5159227766314771037)
XLA Ops:
  0.6 54.2 %shard_map.67 = (bf16[2,4,32,1024]{3,2,1,0:T(8,128)(2,1)}, f32[27,2048]{1,0:T(8,128)}, f32[27,8192]{1,0:T(8,128)}) custom-call(bf16[2,4,32,1024]{3,2,1,0:T(8,128)(2,1)} %x_hbm.1, bf16[27,2048]{1,0:T(8,128)(2,1)} %wa_hbm.1, bf16[27,8192]{1,0:T(8,128)(2,1)} %wb_hbm.1, bf16[2,1,8,1024]{3,2,1,0:T(8,128)(2,1)} %cot_hbm.1), custom_call_target="tpu_custom_call" | custom-call | tf_op jit(solution)/shard_map/pallas_call | solution.py:578
  54.8 2.3 %shard_map.68 = (bf16[2,4,32,1024]{3,2,1,0:T(8,128)(2,1)}, f32[27,2048]{1,0:T(8,128)}, f32[27,8192]{1,0:T(8,128)}) custom-call(bf16[2,4,32,1024]{3,2,1,0:T(8,128)(2,1)} %get-tuple-element.6.dx_in, f32[27,2048]{1,0:T(8,128)} %get-tuple-element.7.ga_in, f32[27,8192]{1,0:T(8,128)} %get-tuple-element.8.gb_in), custom_call_target="tpu_custom_call" | custom-call | tf_op jit(solution)/shard_map/pallas_call | solution.py:626

commit v4 on v3

--- a/solution.py
+++ b/solution.py
@@ -96,17 +96,26 @@
     for load in loads:
         load.start()
 
-    def halo(stage, low_plane, high_plane, landing):
+    def halo(stage, low_plane, high_plane, landing, start=True):
         pair = []
         for way, (src, peer) in enumerate(((high_plane, high), (low_plane, low))):
             copy = pltpu.make_async_remote_copy(
-                src_ref=src, dst_ref=landing.at[way],
+                src_ref=src, dst_ref=landing(way),
                 send_sem=halo_s.at[stage, way], recv_sem=halo_r.at[stage, way],
                 device_id=(me_s, peer), device_id_type=MESH,
             )
-            copy.start()
+            if start:
+                copy.start()
             pair.append(copy)
         return pair
+
+    def pooled_piece(kt, start):
+        w = lanes(384 * kt, 384)
+        return halo(2 + kt, pb.at[:, 1, 1, :, w], pb.at[:, 2, 1, :, w], lambda way: ph.at[way, :, :, w], start)
+
+    def grad_piece(kt, start):
+        w = lanes(768 * kt, 768)
+        return halo(5 + kt, ga.at[:, 1, 16:48, w], ga.at[:, ZD, 16:48, w], lambda way: gh.at[way, :, :, w], start)
 
     half = iota((27, 128), 1) < C2
     loads[0].wait()
@@ -125,7 +134,7 @@
         wb32[pl.ds(i, 27, stride=C2), :] = wb_ref[:, lanes(128 * i, 128)].astype(F32)
 
     pl.semaphore_wait(barrier, 2 * n_gz + n_s - 3)
-    halo_x = halo(0, x_hbm.at[:, 0], x_hbm.at[:, ZD - 1], xh)
+    halo_x = halo(0, x_hbm.at[:, 0], x_hbm.at[:, ZD - 1], lambda way: xh.at[way])
 
     zero_a = jnp.zeros((C1, 128), BF16)
     zero_b = jnp.zeros((C2, 128), BF16)
@@ -211,7 +220,9 @@
             for dy, v in enumerate((rows_before(pooled), pooled, rows_after(pooled))):
                 pb[:, 1:3, dy, :, lanes(128 * kk, 128)] = v.astype(BF16).reshape(CUBES, 2, 16, 128)
 
-    halo_p = halo(1, pb.at[:, 1, 1], pb.at[:, 2, 1], ph)
+        pooled_piece(kt, True)
+
+    halo_p = [copy for kt in range(3) for copy in pooled_piece(kt, False)]
 
     @pl.loop(0, 9)
     def _(zy):
@@ -268,7 +279,7 @@
                 hb[:, 1 + zp, dy, :, 256 + 256 * k:512 + 256 * k] = v.astype(BF16).reshape(CUBES, 16, 256)
         ht[:, 256 * zp:256 * zp + 256] = jnp.concatenate(grads, axis=0).astype(BF16).T
 
-    halo_h = halo(2, hb.at[:, 1, 1, :, 256:2304], hb.at[:, 2, 1, :, 256:2304], hh)
+    halo_h = halo(1, hb.at[:, 1, 1, :, 256:2304], hb.at[:, 2, 1, :, 256:2304], lambda way: hh.at[way])
 
     @pl.loop(0, 3)
     def _(dz):
@@ -439,8 +450,7 @@
     for zp in range(2):
         gp_s[zp] = gp_s[zp] + dot_nt(h_windows((3 * zp,)), tbd[:, 4608 * zp:4608 * zp + 2304])
 
-    @pl.loop(0, BLOCKS)
-    def _(kk):
+    def first_grad(kk):
         up = gp_s[:, pl.ds(pl.multiple_of((kk // 2) * 32, 32), 32), lanes(128 * (kk % 2), 128)]
         up = jnp.concatenate([up, up], axis=2).reshape(2, CUBES, 16, 256)
         g = []
@@ -455,7 +465,15 @@
         for group, v in enumerate((rows_before(odd), even, odd, rows_after(even))):
             ga[:, 1:1 + ZD, 16 * group:16 * group + 16, lanes(256 * kk, 256)] = v.astype(BF16).reshape(CUBES, ZD, 16, 256)
 
-    halo_g = halo(3, ga.at[:, 1, 16:48], ga.at[:, ZD, 16:48], gh)
+    @pl.loop(0, 3)
+    def _(kt):
+        @pl.loop(0, 3)
+        def _(i):
+            first_grad(3 * kt + i)
+
+        grad_piece(kt, True)
+
+    halo_g = [copy for kt in range(3) for copy in grad_piece(kt, False)]
 
     def terms_a(dz):
         window = jnp.concatenate([jnp.concatenate([
@@ -614,7 +632,7 @@
             pltpu.VMEM((n_s, ROWS_A // n_gz, 128), BF16),
             pltpu.VMEM((ROWS_A, 128), BF16),
             dma((4,)), dma((3,)),
-            dma((4, 2)), dma((4, 2)), dma((2,)), dma((2,)),
+            dma((8, 2)), dma((8, 2)), dma((2,)), dma((2,)),
             dma((2, n_gz)), dma((2, n_gz)),
             dma((2, n_s)), dma((2, n_s)),
             dma((2, n_gz)), dma((2, n_gz)),

time: 57.3 us -> 56.6 us (0.988)
  Pallas kernels: 56.5 us -> 55.8 us
    pallas_call x1, Pallas kernels: 54.2 us -> 53.5 us  [shards(): pl.pallas_call(functools.partial(kernel, n_s, n_gz), out_shape=outs, in_s...]
where the time goes in v4:
time: 56.6 us; the launch traced here: 56.5 us
  Pallas kernels  55.8 us (99%)
  between operations  0.64 us (1%)
    pallas_call x1, Pallas kernels, shards(): pl.pallas_call(functools.partial(kernel, n_s, n_gz), out_shape=outs, in_s...  53.5 us
    pallas_call x1, Pallas kernels, shards(): pl.pallas_call(pass_on, out_shape=outs, in_specs=[anywhere] * 3, out_spec...  2.34 us

profile of v4, /device:TPU:1, one launch (start us, length us, event | category | flops | bytes accessed | tf_op | source)
XLA Modules:
  0.0 56.5 jit_solution(17962505829539596301)
XLA Ops:
  0.6 53.5 %shard_map.67 = (bf16[2,4,32,1024]{3,2,1,0:T(8,128)(2,1)}, f32[27,2048]{1,0:T(8,128)}, f32[27,8192]{1,0:T(8,128)}) custom-call(bf16[2,4,32,1024]{3,2,1,0:T(8,128)(2,1)} %x_hbm.1, bf16[27,2048]{1,0:T(8,128)(2,1)} %wa_hbm.1, bf16[27,8192]{1,0:T(8,128)(2,1)} %wb_hbm.1, bf16[2,1,8,1024]{3,2,1,0:T(8,128)(2,1)} %cot_hbm.1), custom_call_target="tpu_custom_call" | custom-call | tf_op jit(solution)/shard_map/pallas_call | solution.py:596
  54.1 2.3 %shard_map.68 = (bf16[2,4,32,1024]{3,2,1,0:T(8,128)(2,1)}, f32[27,2048]{1,0:T(8,128)}, f32[27,8192]{1,0:T(8,128)}) custom-call(bf16[2,4,32,1024]{3,2,1,0:T(8,128)(2,1)} %get-tuple-element.6.dx_in, f32[27,2048]{1,0:T(8,128)} %get-tuple-element.7.ga_in, f32[27,8192]{1,0:T(8,128)} %get-tuple-element.8.gb_in), custom_call_target="tpu_custom_call" | custom-call | tf_op jit(solution)/shard_map/pallas_call | solution.py:644

commit v5 on v4

--- a/solution.py
+++ b/solution.py
@@ -281,8 +281,7 @@
 
     halo_h = halo(1, hb.at[:, 1, 1, :, 256:2304], hb.at[:, 2, 1, :, 256:2304], lambda way: hh.at[way])
 
-    @pl.loop(0, 3)
-    def _(dz):
+    for dz in range(3):
         window = jnp.concatenate([jnp.concatenate([
             pb[:, dz + zp, dy, :, 128 * k:128 * k + 256].reshape(32, 256) for zp in range(2) for k in range(8)
         ], axis=0) for dy in range(3)], axis=1)
@@ -290,7 +289,7 @@
         for dy in range(3):
             full = all_dy[:, 256 * dy:256 * dy + 256]
             diag = full[:128] + pltpu.roll(full[128:], 192, 1)
-            sb[pl.ds(pl.multiple_of(dz * 576 + dy * 192, 64), 192), :] = diag.astype(BF16).T[:192]
+            sb[dz * 576 + dy * 192:dz * 576 + dy * 192 + 192, :] = diag.astype(BF16).T[:192]
 
     sb[1728:ROWS_B, :] = jnp.zeros((ROWS_B - 1728, 128), BF16)
     hs[HALF_B:, :] = jnp.zeros((WIDE_B - HALF_B, 128), BF16)
@@ -477,7 +476,7 @@
 
     def terms_a(dz):
         window = jnp.concatenate([jnp.concatenate([
-            xa[:, pl.ds(dz, ZD), 16 * dy:16 * dy + 32, 128 * kk:128 * kk + 256].reshape(256, 256)
+            xa[:, dz:dz + ZD, 16 * dy:16 * dy + 32, 128 * kk:128 * kk + 256].reshape(256, 256)
             for kk in range(BLOCKS)
         ], axis=0) for dy in range(3)], axis=1)
         all_dy = dot(gt[...], window)
@@ -490,10 +489,9 @@
                     at = 128 * par + 64 * pair
                     total = total + pltpu.roll(full[at:at + 64], 256 - 32 * (t + 1), 1)
             total = total[:, :128]
-            da[pl.ds(pl.multiple_of(dz * 288 + dy * 96, 32), 96), :] = jnp.concatenate([total, total], axis=0).T[:96]
-
-    @pl.loop(0, 3)
-    def _(dz):
+            da[dz * 288 + dy * 96:dz * 288 + dy * 96 + 96, :] = jnp.concatenate([total, total], axis=0).T[:96]
+
+    for dz in range(3):
         terms_a(dz)
 
     half = iota((ROWS_A, 128), 1) < C2
@@ -549,7 +547,7 @@
 
     @pl.loop(0, C2)
     def _(i):
-        gb_ref[:, lanes(128 * i, 128)] = wb32[pl.ds(i, 27, stride=C2), :]
+        gb_ref[:, lanes(128 * i, 128)] = wb32[pl.ds(i, 27, stride=C2), :].astype(BF16)
 
     store(gb_ref, gb_hbm)
     wait_all(functools.partial(gather_copy, 1, fa), n_gz)
@@ -568,17 +566,23 @@
         copy.wait()
 
 
-def pass_on(dx_in, ga_in, gb_in, dx_out, ga_out, gb_out, dx_ref, ga_ref, gb_ref, in_s, out_s):
+def pass_on(dx_in, ga_in, gb_in, dx_out, ga_out, gb_out, dx_ref, ga_ref, gb_ref, wide_ref, in_s, out_s):
     near, far = pl.ds(0, 4096), pl.ds(4096, 4096)
     pieces = [(dx_in.at[b], dx_ref.at[b], dx_out.at[b]) for b in range(CUBES)]
-    pieces += [(gb_in.at[:, w], gb_ref.at[:, w], gb_out.at[:, w]) for w in (near, far)]
+    pieces += [(gb_in.at[:, w], wide_ref.at[:, w], gb_out.at[:, w]) for w in (near, far)]
     pieces.append((ga_in, ga_ref, ga_out))
-    taken = [pltpu.make_async_copy(src, via, in_s.at[i]) for i, (src, via, _) in enumerate(pieces)]
     given = [pltpu.make_async_copy(via, dst, out_s.at[i]) for i, (_, via, dst) in enumerate(pieces)]
+    narrow = {2: near, 3: far}
+    taken = [
+        pltpu.make_async_copy(src, gb_ref.at[:, narrow[i]] if i in narrow else via, in_s.at[i])
+        for i, (src, via, _) in enumerate(pieces)
+    ]
     for copy in taken:
         copy.start()
-    for arrive, leave in zip(taken, given):
+    for i, (arrive, leave) in enumerate(zip(taken, given)):
         arrive.wait()
+        if i in narrow:
+            wide_ref[:, narrow[i]] = gb_ref[:, narrow[i]].astype(F32)
         leave.start()
     for copy in given:
         copy.wait()
@@ -593,12 +597,13 @@
         jax.ShapeDtypeStruct((27, C1 * C2), F32),
         jax.ShapeDtypeStruct((27, C2 * C3), F32),
     )
+    parts = outs[:2] + (jax.ShapeDtypeStruct((27, C2 * C3), BF16),)
     results = pl.pallas_call(
         functools.partial(kernel, n_s, n_gz),
-        out_shape=outs,
+        out_shape=parts,
         in_specs=[anywhere] * 4,
         out_specs=(anywhere,) * 3,
-        scratch_shapes=[pltpu.VMEM(v.shape, v.dtype) for v in ins + outs] + [
+        scratch_shapes=[pltpu.VMEM(v.shape, v.dtype) for v in ins + parts] + [
             pltpu.VMEM((27 * C1, 128), F32),
             pltpu.VMEM((ROWS_B, 128), F32),
             pltpu.VMEM((CUBES, ZD + 2, 64, 1280), BF16),
@@ -646,7 +651,7 @@
         out_shape=outs,
         in_specs=[anywhere] * 3,
         out_specs=(anywhere,) * 3,
-        scratch_shapes=[pltpu.VMEM(v.shape, v.dtype) for v in outs] + [dma((5,)), dma((5,))],
+        scratch_shapes=[pltpu.VMEM(v.shape, v.dtype) for v in parts + outs[2:]] + [dma((5,)), dma((5,))],
     )(*results)
 
 

time: 56.6 us -> 55.8 us (0.986)
  Pallas kernels: 55.8 us -> 55 us
    pallas_call x1, Pallas kernels: 53.5 us -> 52.7 us  [shards(): pl.pallas_call(functools.partial(kernel, n_s, n_gz), out_shape=parts, in_...]
where the time goes in v5:
time: 55.8 us; the launch traced here: 55.6 us
  Pallas kernels  55 us (99%)
  between operations  0.64 us (1%)
    pallas_call x1, Pallas kernels, shards(): pl.pallas_call(functools.partial(kernel, n_s, n_gz), out_shape=parts, in_...  52.7 us
    pallas_call x1, Pallas kernels, shards(): pl.pallas_call(pass_on, out_shape=outs, in_specs=[anywhere] * 3, out_spec...  2.28 us

profile of v5, /device:TPU:1, one launch (start us, length us, event | category | flops | bytes accessed | tf_op | source)
XLA Modules:
  0.0 55.6 jit_solution(1651054150475073090)
XLA Ops:
  0.6 52.7 %shard_map.67 = (bf16[2,4,32,1024]{3,2,1,0:T(8,128)(2,1)}, f32[27,2048]{1,0:T(8,128)}, bf16[27,8192]{1,0:T(8,128)(2,1)}) custom-call(bf16[2,4,32,1024]{3,2,1,0:T(8,128)(2,1)} %x_hbm.1, bf16[27,2048]{1,0:T(8,128)(2,1)} %wa_hbm.1, bf16[27,8192]{1,0:T(8,128)(2,1)} %wb_hbm.1, bf16[2,1,8,1024]{3,2,1,0:T(8,128)(2,1)} %cot_hbm.1), custom_call_target="tpu_custom_call" | custom-call | tf_op jit(solution)/shard_map/pallas_call | solution.py:601
  53.4 2.3 %shard_map.68 = (bf16[2,4,32,1024]{3,2,1,0:T(8,128)(2,1)}, f32[27,2048]{1,0:T(8,128)}, f32[27,8192]{1,0:T(8,128)}) custom-call(bf16[2,4,32,1024]{3,2,1,0:T(8,128)(2,1)} %get-tuple-element.6.dx_in, f32[27,2048]{1,0:T(8,128)} %get-tuple-element.7.ga_in, bf16[27,8192]{1,0:T(8,128)(2,1)} %get-tuple-element.8.gb_in), custom_call_target="tpu_custom_call" | custom-call | tf_op jit(solution)/shard_map/pallas_call | solution.py:649

commit v6 on v5

--- a/solution.py
+++ b/solution.py
@@ -604,8 +604,8 @@
         in_specs=[anywhere] * 4,
         out_specs=(anywhere,) * 3,
         scratch_shapes=[pltpu.VMEM(v.shape, v.dtype) for v in ins + parts] + [
-            pltpu.VMEM((27 * C1, 128), F32),
-            pltpu.VMEM((ROWS_B, 128), F32),
+            pltpu.VMEM((32 * C1, 128), F32),
+            pltpu.VMEM((32 * C2, 128), F32),
             pltpu.VMEM((CUBES, ZD + 2, 64, 1280), BF16),
             pltpu.VMEM((2304, 256), BF16),
             pltpu.VMEM((2304, 256), BF16),

time: 55.8 us -> 55.8 us (level)
  no operation moved by 1% of the time
where the time goes in v6:
time: 55.8 us; the launch traced here: 55.6 us
  Pallas kernels  55 us (99%)
  between operations  0.64 us (1%)
    pallas_call x1, Pallas kernels, shards(): pl.pallas_call(functools.partial(kernel, n_s, n_gz), out_shape=parts, in_...  52.7 us
    pallas_call x1, Pallas kernels, shards(): pl.pallas_call(pass_on, out_shape=outs, in_specs=[anywhere] * 3, out_spec...  2.28 us

profile of v6, /device:TPU:1, one launch (start us, length us, event | category | flops | bytes accessed | tf_op | source)
XLA Modules:
  0.0 55.6 jit_solution(13042560271736443073)
XLA Ops:
  0.6 52.7 %shard_map.67 = (bf16[2,4,32,1024]{3,2,1,0:T(8,128)(2,1)}, f32[27,2048]{1,0:T(8,128)}, bf16[27,8192]{1,0:T(8,128)(2,1)}) custom-call(bf16[2,4,32,1024]{3,2,1,0:T(8,128)(2,1)} %x_hbm.1, bf16[27,2048]{1,0:T(8,128)(2,1)} %wa_hbm.1, bf16[27,8192]{1,0:T(8,128)(2,1)} %wb_hbm.1, bf16[2,1,8,1024]{3,2,1,0:T(8,128)(2,1)} %cot_hbm.1), custom_call_target="tpu_custom_call" | custom-call | tf_op jit(solution)/shard_map/pallas_call | solution.py:601
  53.4 2.3 %shard_map.68 = (bf16[2,4,32,1024]{3,2,1,0:T(8,128)(2,1)}, f32[27,2048]{1,0:T(8,128)}, f32[27,8192]{1,0:T(8,128)}) custom-call(bf16[2,4,32,1024]{3,2,1,0:T(8,128)(2,1)} %get-tuple-element.6.dx_in, f32[27,2048]{1,0:T(8,128)} %get-tuple-element.7.ga_in, bf16[27,8192]{1,0:T(8,128)(2,1)} %get-tuple-element.8.gb_in), custom_call_target="tpu_custom_call" | custom-call | tf_op jit(solution)/shard_map/pallas_call | solution.py:649
